TPU v7x, 256 devices: a whole 4x4x8 slice. The times are simulated.
256 devices in a mesh: grid: 16 (over z, y_lo), chan: 16 (over x, y_hi, core).
Axes of the slice: x: 4, y: 4 (y_hi: 2, y_lo: 2; y = y_hi * 2 + y_lo), z: 8, core: 2. Of those that a mesh axis runs over, the one named last changes fastest.
Arguments:
- spectra: bfloat16 [2, 8, 48, 4096], P(None, None, 'grid', 'chan'), may hold values from -90 to 90, as said below
- travel: int32 [65536, 4096], P('grid', 'chan'), may hold values from 0 to 2047
- quality: int32 [4096], P('chan'), may hold values 0 or 1
Outputs:
- beam_power: float32 [48, 65536], P(None, ('grid', 'chan'))
Inputs may be any that keep to these rules, and one draw needn't show every extreme that they name: `spectra`: spectra of the windows; scales differ between channels and between windows.
All inputs are finite; a program needn't handle non-finite values. No bound on the sum of `quality` on one device may be relied on, other than what follows from the above.
Results may differ from a plain program's by a relative error of at most 0.0012.
Values may be sent and summed in bfloat16 or wider, within the bound.
No kernel may reach another device: no remote copies, remote signals or barrier semaphores. Data moves between devices by JAX's collectives and lax.ppermute only.
A program may use at most 64 MiB of HBM per device.

v0:
```python
import math
import jax
import jax.numpy as jnp
from jax import lax
from jax.sharding import PartitionSpec as P

NFFT = 2048
lowest_bin = 37
bin_spacing = 29


def replica_rows(delay_rows, freq_count):
    freq_bins = lowest_bin + bin_spacing * jnp.arange(freq_count, dtype=jnp.int32)
    phase_index = freq_bins[:, None, None] * delay_rows[None, :, :] % NFFT
    angles = phase_index.astype(jnp.float32) * (2.0 * math.pi / NFFT)
    return jnp.concatenate([jnp.cos(angles), jnp.sin(angles)], axis=2).astype(jnp.bfloat16)


def stacked_spectra(masked):
    real_part = masked[0]
    imag_part = masked[1]
    upper_half = jnp.concatenate([real_part, imag_part], axis=1)
    lower_half = jnp.concatenate([-imag_part, real_part], axis=1)
    return jnp.concatenate([upper_half, lower_half], axis=2)


def beams_for(delay_table, spectra_matrix, freq_count):
    total_rows = delay_table.shape[0]
    chan_width = delay_table.shape[1]
    block_rows = math.gcd(total_rows, 1024)

    def one_block(delay_rows):
        replicas = replica_rows(delay_rows, freq_count)
        beam_terms = jnp.einsum(
            "frk,fwk->rfw", replicas, spectra_matrix, preferred_element_type=jnp.float32
        )
        return beam_terms.reshape(block_rows, -1)

    block_terms = lax.map(
        one_block, delay_table.reshape(total_rows // block_rows, block_rows, chan_width)
    )
    return block_terms.reshape(total_rows, -1)


def per_device(spectra, travel, quality):
    freq_count = spectra.shape[1]
    masked = spectra * quality.astype(jnp.bfloat16)
    channel_count = masked.shape[3] * lax.axis_size("chan")
    gathered = lax.all_gather(masked, "grid", axis=2, tiled=True)
    window_count = gathered.shape[2]
    norm_sum = lax.psum(jnp.sum(gathered.astype(jnp.float32) ** 2, axis=(0, 1, 3)), "chan")
    window_norm = norm_sum / (freq_count * channel_count) + 1e-06
    rows_out = travel.shape[0] // lax.axis_size("chan")
    spectra_matrix = stacked_spectra(gathered)
    beam_sums = lax.psum_scatter(
        beams_for(travel, spectra_matrix, freq_count), "chan", scatter_dimension=0, tiled=True
    )
    energies = jnp.sum(beam_sums.reshape(rows_out, 2 * freq_count, window_count) ** 2, axis=1)
    beam_power = energies / (freq_count * channel_count * window_norm[None, :])
    return beam_power.T


def solution(mesh):
    return jax.shard_map(
        per_device,
        mesh=mesh,
        in_specs=(P(None, None, "grid", "chan"), P("grid", "chan"), P("chan")),
        out_specs=P(None, ("grid", "chan")),
        check_vma=False,
    )
```

profile of v0, /device:TPU:1, one launch (start us, length us, event | category | flops | bytes accessed | tf_op | source)
XLA Modules:
  0.0 362.6 jit_solution(12810021472243952818)
XLA Ops:
  6.5 0.7 convert_element_type.16
  7.2 0.7 copy_multiply_fusion
  8.0 32.6 %all_gather.3 = bf16[2,8,48,256]{3,1,0,2:T(8,128)(2,1)S(1)} all-gather(bf16[2,8,3,256]{3,1,0,2:T(8,128)(2,1)S(1)} %copy_multiply_fusion), channel_id=1, replica_groups=mesh['grid'=16,'chan'=16] {'grid'}, dimensions={2}, use_global_device_ids=true | all-gather | bytes 417792 | tf_op jit(solution)/shard_map/all_gather | solution.py:49
  40.6 0.1 maximum_maximum_fusion
  40.7 1.1 copy.10
  41.8 177.9 %while.12 = (s32[]{:T(128)}, f32[4,1024,768]{2,1,0:T(8,128)}, s32[4,1024,256]{2,1,0:T(8,128)}, bf16[8,96,512]{2,1,0:T(8,128)(2,1)}, s32[]{:T(128)}) while((s32[]{:T(128)}, f32[4,1024,768]{2,1,0:T(8,128)}, s32[4,1024,256]{2,1,0:T(8,128)}, bf16[8,96,512]{2,1,0:T(8,128)(2,1)}, s32[]{:T(128)}) %tuple.36), condition=%wide.region_1.0_spmd, body=%wide.region_0.0_spmd.sunk | while | flops 855638016 | bytes 36438156 | solution.py:39
  41.8 1.3 dynamic-slice_bitcast_fusion.2
  43.1 33.8 %cosine_convert_fusion.2 = (bf16[8,1024,256]{2,1,0:T(8,128)(2,1)S(1)}, bf16[8,1024,256]{2,1,0:T(8,128)(2,1)S(1)}) fusion(s32[1024,256]{1,0:T(8,128)S(1)} %dynamic-slice_bitcast_fusion.2, s32[8]{0:T(128)S(1)} %multiply_add_fusion.2), kind=kLoop, calls=%fused_computation.13.clone.1 | loop fusion | flops 33554432 | bytes 9437216 | tf_op jit(solution)/shard_map/convert
  76.9 5.1 %fusion.15 = f32[8,1024,96]{1,2,0:T(8,128)} fusion(bf16[8,96,512]{2,1,0:T(8,128)(2,1)} %get-tuple-element.118, bf16[8,1024,256]{2,1,0:T(8,128)(2,1)S(1)} %get-tuple-element.103, bf16[8,1024,256]{2,1,0:T(8,128)(2,1)S(1)} %get-tuple-element.104), kind=kOutput, calls=%fused_computation.8.clone.1 | convolution fusion | flops 822083584 | bytes 12320768 | tf_op jit(solution)/shard_map/while/body/eval_jaxpr/frk,fwk->rfw/dot_general | solution.py:34
  82.0 2.4 copy.20
  84.4 1.9 constant_dynamic-update-slice_fusion.2
  86.3 1.3 dynamic-slice_bitcast_fusion.2
  87.6 33.8 %cosine_convert_fusion.2 = (bf16[8,1024,256]{2,1,0:T(8,128)(2,1)S(1)}, bf16[8,1024,256]{2,1,0:T(8,128)(2,1)S(1)}) fusion(s32[1024,256]{1,0:T(8,128)S(1)} %dynamic-slice_bitcast_fusion.2, s32[8]{0:T(128)S(1)} %multiply_add_fusion.2), kind=kLoop, calls=%fused_computation.13.clone.1 | loop fusion | flops 33554432 | bytes 9437216 | tf_op jit(solution)/shard_map/convert
  121.4 5.1 %fusion.15 = f32[8,1024,96]{1,2,0:T(8,128)} fusion(bf16[8,96,512]{2,1,0:T(8,128)(2,1)} %get-tuple-element.118, bf16[8,1024,256]{2,1,0:T(8,128)(2,1)S(1)} %get-tuple-element.103, bf16[8,1024,256]{2,1,0:T(8,128)(2,1)S(1)} %get-tuple-element.104), kind=kOutput, calls=%fused_computation.8.clone.1 | convolution fusion | flops 822083584 | bytes 12320768 | tf_op jit(solution)/shard_map/while/body/eval_jaxpr/frk,fwk->rfw/dot_general | solution.py:34
  126.5 2.4 copy.20
  128.9 1.9 constant_dynamic-update-slice_fusion.2
  130.8 1.3 dynamic-slice_bitcast_fusion.2
  132.1 33.8 %cosine_convert_fusion.2 = (bf16[8,1024,256]{2,1,0:T(8,128)(2,1)S(1)}, bf16[8,1024,256]{2,1,0:T(8,128)(2,1)S(1)}) fusion(s32[1024,256]{1,0:T(8,128)S(1)} %dynamic-slice_bitcast_fusion.2, s32[8]{0:T(128)S(1)} %multiply_add_fusion.2), kind=kLoop, calls=%fused_computation.13.clone.1 | loop fusion | flops 33554432 | bytes 9437216 | tf_op jit(solution)/shard_map/convert
  165.9 5.1 %fusion.15 = f32[8,1024,96]{1,2,0:T(8,128)} fusion(bf16[8,96,512]{2,1,0:T(8,128)(2,1)} %get-tuple-element.118, bf16[8,1024,256]{2,1,0:T(8,128)(2,1)S(1)} %get-tuple-element.103, bf16[8,1024,256]{2,1,0:T(8,128)(2,1)S(1)} %get-tuple-element.104), kind=kOutput, calls=%fused_computation.8.clone.1 | convolution fusion | flops 822083584 | bytes 12320768 | tf_op jit(solution)/shard_map/while/body/eval_jaxpr/frk,fwk->rfw/dot_general | solution.py:34
  171.0 2.4 copy.20
  173.4 1.9 constant_dynamic-update-slice_fusion.2
  175.3 1.3 dynamic-slice_bitcast_fusion.2
  176.6 33.8 %cosine_convert_fusion.2 = (bf16[8,1024,256]{2,1,0:T(8,128)(2,1)S(1)}, bf16[8,1024,256]{2,1,0:T(8,128)(2,1)S(1)}) fusion(s32[1024,256]{1,0:T(8,128)S(1)} %dynamic-slice_bitcast_fusion.2, s32[8]{0:T(128)S(1)} %multiply_add_fusion.2), kind=kLoop, calls=%fused_computation.13.clone.1 | loop fusion | flops 33554432 | bytes 9437216 | tf_op jit(solution)/shard_map/convert
  210.4 5.1 %fusion.15 = f32[8,1024,96]{1,2,0:T(8,128)} fusion(bf16[8,96,512]{2,1,0:T(8,128)(2,1)} %get-tuple-element.118, bf16[8,1024,256]{2,1,0:T(8,128)(2,1)S(1)} %get-tuple-element.103, bf16[8,1024,256]{2,1,0:T(8,128)(2,1)S(1)} %get-tuple-element.104), kind=kOutput, calls=%fused_computation.8.clone.1 | convolution fusion | flops 822083584 | bytes 12320768 | tf_op jit(solution)/shard_map/while/body/eval_jaxpr/frk,fwk->rfw/dot_general | solution.py:34
  215.5 2.4 copy.20
  217.9 1.8 constant_dynamic-update-slice_fusion.2
  219.7 0.4 multiply_reduce_fusion
  220.2 39.9 %psum.7 = f32[48]{0:T(128)S(1)} all-reduce(f32[48]{0:T(128)S(1)} %multiply_reduce_fusion), channel_id=1, replica_groups=mesh['grid'=16,'chan'=16] {'chan'}, use_global_device_ids=true, to_apply=%region_5.6 | all-reduce | flops 48 | bytes 384 | tf_op jit(solution)/shard_map/psum | solution.py:51
  260.1 93.1 %reduce-scatter.2.cloned.1.call-done = f32[256,768]{1,0:T(8,128)} async-done(((f32[4096,768]{1,0:T(8,128)}), f32[256,768]{1,0:T(8,128)}) %reduce-scatter.2.cloned.1.call-update) | async-done | bytes 786448 | tf_op jit(solution)/shard_map/reduce_scatter | solution.py:55
  353.3 1.5 integer_pow.9
  354.7 0.3 copy.12
  355.1 0.7 divide_bitcast_fusion
  (11 shorter events, 0.1 us)
Async XLA Ops:
  6.5 346.7 %reduce-scatter.2.cloned.1.call-start = ((), (), s32[]{:S(2)}) async-start(), calls=%async_computation.1 | async-start | bytes 13369344 | tf_op jit(solution)/shard_map/reduce_scatter | solution.py:55
Sparse Core Ops, SparseCore 0:
  219.9 133.3 reduce-scatter.1
where the time goes:
time: 363 us
  other arithmetic  139 us (38%)
  waiting for transfers between devices  93.2 us (26%)
  blocking collectives  72.5 us (20%)
  local copies, waits for them, and re-layouts  23.6 us (7%)
  matrix products  20.4 us (6%)
  between operations  13.4 us (4%)
    another operation x4, other arithmetic  135 us
    reduce_scatter x1, waiting for transfers between devices, per_device(): lax.psum_scatter(beams_for(travel, spectra_matrix, freq_count), 'chan', s...  93.1 us
    psum x1, blocking collectives, per_device(): lax.psum(jnp.sum(gathered.astype(jnp.float32) ** 2, axis=(0, 1, 3)), 'chan')  39.9 us
    all_gather x1, blocking collectives, per_device(): gathered = lax.all_gather(masked, 'grid', axis=2, tiled=True)  32.6 us
    dot_general x4, matrix products, one_block(): jnp.einsum('frk,fwk->rfw', replicas, spectra_matrix, preferred_element_ty...  20.4 us
    dynamic_update_slice x8, local copies, waits for them, and re-layouts, beams_for(): lax.map(one_block, delay_table.reshape(total_rows // block_rows, block_ro...  17 us
  transfers between devices with their start and end apart: 1, of which 1 were waited for; matrix products, arithmetic and copies ran while one was open for 0% of the time, Pallas kernels for 0%

commit v1 on v0

--- a/solution.py
+++ b/solution.py
@@ -46,7 +46,9 @@
     freq_count = spectra.shape[1]
     masked = spectra * quality.astype(jnp.bfloat16)
     channel_count = masked.shape[3] * lax.axis_size("chan")
-    gathered = lax.all_gather(masked, "grid", axis=2, tiled=True)
+    gathered = jnp.concatenate(
+        lax.all_to_all(jnp.stack([masked] * lax.axis_size("grid")), "grid", 0, 0), axis=2
+    )
     window_count = gathered.shape[2]
     norm_sum = lax.psum(jnp.sum(gathered.astype(jnp.float32) ** 2, axis=(0, 1, 3)), "chan")
     window_norm = norm_sum / (freq_count * channel_count) + 1e-06

time: 363 us -> 349 us (0.961)
  blocking collectives: 72.5 us -> 34.7 us
  waiting for transfers between devices: 93.2 us -> 106 us
  starting transfers between devices: 0.01 us -> 10.2 us
    all_gather x1 -> x0, blocking collectives: 32.6 us -> none  [per_device(): gathered = lax.all_gather(masked, 'grid', axis=2, tiled=True)]
    all_to_all x0 -> x1, waiting for transfers between devices: none -> 13.2 us  [per_device(): lax.all_to_all(jnp.stack([masked] * lax.axis_size('grid')), 'grid', 0, 0)]
    all_to_all x0 -> x1, starting transfers between devices: none -> 10.1 us  [per_device(): lax.all_to_all(jnp.stack([masked] * lax.axis_size('grid')), 'grid', 0, 0)]
    psum x1, blocking collectives: 39.9 us -> 34.7 us  [per_device(): lax.psum(jnp.sum(gathered.astype(jnp.float32) ** 2, axis=(0, 1, 3)), 'chan')]
  transfers between devices with their start and end apart: 1 -> 2, of which waited for: 1 -> 2; matrix products, arithmetic and copies ran while one was open for 0% -> 0% of each run, Pallas kernels for 0% -> 0%
where the time goes in v1:
time: 349 us
  other arithmetic  139 us (40%)
  waiting for transfers between devices  106 us (30%)
  blocking collectives  34.7 us (10%)
  local copies, waits for them, and re-layouts  24.5 us (7%)
  matrix products  20.4 us (6%)
  between operations  13.5 us (4%)
  starting transfers between devices  10.2 us (3%)
    another operation x4, other arithmetic  135 us
    reduce_scatter x1, waiting for transfers between devices, per_device(): lax.psum_scatter(beams_for(travel, spectra_matrix, freq_count), 'chan', s...  92.9 us
    psum x1, blocking collectives, per_device(): lax.psum(jnp.sum(gathered.astype(jnp.float32) ** 2, axis=(0, 1, 3)), 'chan')  34.7 us
    dot_general x4, matrix products, one_block(): jnp.einsum('frk,fwk->rfw', replicas, spectra_matrix, preferred_element_ty...  20.4 us
    dynamic_update_slice x8, local copies, waits for them, and re-layouts, beams_for(): lax.map(one_block, delay_table.reshape(total_rows // block_rows, block_ro...  17 us
    all_to_all x1, waiting for transfers between devices, per_device(): lax.all_to_all(jnp.stack([masked] * lax.axis_size('grid')), 'grid', 0, 0)  13.2 us
    all_to_all x1, starting transfers between devices, per_device(): lax.all_to_all(jnp.stack([masked] * lax.axis_size('grid')), 'grid', 0, 0)  10.1 us
  transfers between devices with their start and end apart: 2, of which 2 were waited for; matrix products, arithmetic and copies ran while one was open for 0% of the time, Pallas kernels for 0%

profile of v1, /device:TPU:1, one launch (start us, length us, event | category | flops | bytes accessed | tf_op | source)
XLA Modules:
  0.0 348.6 jit_solution(12883207758132385941)
XLA Ops:
  6.5 0.7 convert_element_type.17
  7.2 0.7 broadcast_multiply_fusion
  8.0 0.8 stack.2
  8.8 10.1 %all-to-all-start = ((bf16[16,2,8,3,256]{4,2,3,1,0:T(8,128)(2,1)}), bf16[16,2,8,3,256]{4,2,3,1,0:T(8,128)(2,1)S(1)}, u32[]{:S(2)}, u32[]{:S(2)}) async-start(bf16[16,2,8,3,256]{4,2,3,1,0:T(8,128)(2,1)} %stack.2), calls=%async_computation | async-start | bytes 786432 | tf_op jit(solution)/shard_map/all_to_all | solution.py:50
  19.0 13.2 %all-to-all-done = bf16[16,2,8,3,256]{4,2,3,1,0:T(8,128)(2,1)S(1)} async-done(((bf16[16,2,8,3,256]{4,2,3,1,0:T(8,128)(2,1)}), bf16[16,2,8,3,256]{4,2,3,1,0:T(8,128)(2,1)S(1)}, u32[]{:S(2)}, u32[]{:S(2)}) %all-to-all-start) | async-done | bytes 393248 | tf_op jit(solution)/shard_map/all_to_all | solution.py:50
  32.4 1.1 copy.9
  33.5 177.9 %while.12 = (s32[]{:T(128)}, f32[4,1024,768]{2,1,0:T(8,128)}, s32[4,1024,256]{2,1,0:T(8,128)}, bf16[8,96,512]{2,1,0:T(8,128)(2,1)}, s32[]{:T(128)}) while((s32[]{:T(128)}, f32[4,1024,768]{2,1,0:T(8,128)}, s32[4,1024,256]{2,1,0:T(8,128)}, bf16[8,96,512]{2,1,0:T(8,128)(2,1)}, s32[]{:T(128)}) %tuple.37), condition=%wide.region_1.0_spmd, body=%wide.region_0.0_spmd.sunk | while | flops 855638016 | bytes 36438156 | solution.py:39
  33.5 1.3 dynamic-slice_bitcast_fusion.2
  34.8 33.8 %cosine_convert_fusion.2 = (bf16[8,1024,256]{2,1,0:T(8,128)(2,1)S(1)}, bf16[8,1024,256]{2,1,0:T(8,128)(2,1)S(1)}) fusion(s32[1024,256]{1,0:T(8,128)S(1)} %dynamic-slice_bitcast_fusion.2, s32[8]{0:T(128)S(1)} %multiply_add_fusion.2), kind=kLoop, calls=%fused_computation.13.clone.1 | loop fusion | flops 33554432 | bytes 9437216 | tf_op jit(solution)/shard_map/convert
  68.6 5.1 %fusion.15 = f32[8,1024,96]{1,2,0:T(8,128)} fusion(bf16[8,96,512]{2,1,0:T(8,128)(2,1)} %get-tuple-element.122, bf16[8,1024,256]{2,1,0:T(8,128)(2,1)S(1)} %get-tuple-element.107, bf16[8,1024,256]{2,1,0:T(8,128)(2,1)S(1)} %get-tuple-element.108), kind=kOutput, calls=%fused_computation.8.clone.1 | convolution fusion | flops 822083584 | bytes 12320768 | tf_op jit(solution)/shard_map/while/body/eval_jaxpr/frk,fwk->rfw/dot_general | solution.py:34
  73.7 2.4 copy.21
  76.1 1.9 constant_dynamic-update-slice_fusion.2
  78.0 1.3 dynamic-slice_bitcast_fusion.2
  79.3 33.8 %cosine_convert_fusion.2 = (bf16[8,1024,256]{2,1,0:T(8,128)(2,1)S(1)}, bf16[8,1024,256]{2,1,0:T(8,128)(2,1)S(1)}) fusion(s32[1024,256]{1,0:T(8,128)S(1)} %dynamic-slice_bitcast_fusion.2, s32[8]{0:T(128)S(1)} %multiply_add_fusion.2), kind=kLoop, calls=%fused_computation.13.clone.1 | loop fusion | flops 33554432 | bytes 9437216 | tf_op jit(solution)/shard_map/convert
  113.1 5.1 %fusion.15 = f32[8,1024,96]{1,2,0:T(8,128)} fusion(bf16[8,96,512]{2,1,0:T(8,128)(2,1)} %get-tuple-element.122, bf16[8,1024,256]{2,1,0:T(8,128)(2,1)S(1)} %get-tuple-element.107, bf16[8,1024,256]{2,1,0:T(8,128)(2,1)S(1)} %get-tuple-element.108), kind=kOutput, calls=%fused_computation.8.clone.1 | convolution fusion | flops 822083584 | bytes 12320768 | tf_op jit(solution)/shard_map/while/body/eval_jaxpr/frk,fwk->rfw/dot_general | solution.py:34
  118.2 2.4 copy.21
  120.6 1.9 constant_dynamic-update-slice_fusion.2
  122.5 1.3 dynamic-slice_bitcast_fusion.2
  123.8 33.8 %cosine_convert_fusion.2 = (bf16[8,1024,256]{2,1,0:T(8,128)(2,1)S(1)}, bf16[8,1024,256]{2,1,0:T(8,128)(2,1)S(1)}) fusion(s32[1024,256]{1,0:T(8,128)S(1)} %dynamic-slice_bitcast_fusion.2, s32[8]{0:T(128)S(1)} %multiply_add_fusion.2), kind=kLoop, calls=%fused_computation.13.clone.1 | loop fusion | flops 33554432 | bytes 9437216 | tf_op jit(solution)/shard_map/convert
  157.6 5.1 %fusion.15 = f32[8,1024,96]{1,2,0:T(8,128)} fusion(bf16[8,96,512]{2,1,0:T(8,128)(2,1)} %get-tuple-element.122, bf16[8,1024,256]{2,1,0:T(8,128)(2,1)S(1)} %get-tuple-element.107, bf16[8,1024,256]{2,1,0:T(8,128)(2,1)S(1)} %get-tuple-element.108), kind=kOutput, calls=%fused_computation.8.clone.1 | convolution fusion | flops 822083584 | bytes 12320768 | tf_op jit(solution)/shard_map/while/body/eval_jaxpr/frk,fwk->rfw/dot_general | solution.py:34
  162.7 2.4 copy.21
  165.1 1.9 constant_dynamic-update-slice_fusion.2
  167.0 1.3 dynamic-slice_bitcast_fusion.2
  168.3 33.8 %cosine_convert_fusion.2 = (bf16[8,1024,256]{2,1,0:T(8,128)(2,1)S(1)}, bf16[8,1024,256]{2,1,0:T(8,128)(2,1)S(1)}) fusion(s32[1024,256]{1,0:T(8,128)S(1)} %dynamic-slice_bitcast_fusion.2, s32[8]{0:T(128)S(1)} %multiply_add_fusion.2), kind=kLoop, calls=%fused_computation.13.clone.1 | loop fusion | flops 33554432 | bytes 9437216 | tf_op jit(solution)/shard_map/convert
  202.1 5.1 %fusion.15 = f32[8,1024,96]{1,2,0:T(8,128)} fusion(bf16[8,96,512]{2,1,0:T(8,128)(2,1)} %get-tuple-element.122, bf16[8,1024,256]{2,1,0:T(8,128)(2,1)S(1)} %get-tuple-element.107, bf16[8,1024,256]{2,1,0:T(8,128)(2,1)S(1)} %get-tuple-element.108), kind=kOutput, calls=%fused_computation.8.clone.1 | convolution fusion | flops 822083584 | bytes 12320768 | tf_op jit(solution)/shard_map/while/body/eval_jaxpr/frk,fwk->rfw/dot_general | solution.py:34
  207.2 2.4 copy.21
  209.6 1.8 constant_dynamic-update-slice_fusion.2
  211.7 34.7 %psum.7 = f32[48]{0:T(128)S(1)} all-reduce(f32[48]{0:T(128)S(1)} %reduce_sum.22), channel_id=1, replica_groups=mesh['grid'=16,'chan'=16] {'chan'}, use_global_device_ids=true, to_apply=%region_5.6 | all-reduce | flops 48 | bytes 384 | tf_op jit(solution)/shard_map/psum | solution.py:53
  246.4 92.9 %reduce-scatter.2.cloned.1.call-done = f32[256,768]{1,0:T(8,128)} async-done(((f32[4096,768]{1,0:T(8,128)}), f32[256,768]{1,0:T(8,128)}) %reduce-scatter.2.cloned.1.call-update) | async-done | bytes 786448 | tf_op jit(solution)/shard_map/reduce_scatter | solution.py:57
  339.3 1.5 integer_pow.10
  340.7 0.3 copy.11
  341.1 0.7 divide_bitcast_fusion
  (15 shorter events, 0.6 us)
Async XLA Ops:
  8.8 23.4 %all-to-all-start = ((bf16[16,2,8,3,256]{4,2,3,1,0:T(8,128)(2,1)}), bf16[16,2,8,3,256]{4,2,3,1,0:T(8,128)(2,1)S(1)}, u32[]{:S(2)}, u32[]{:S(2)}) async-start(bf16[16,2,8,3,256]{4,2,3,1,0:T(8,128)(2,1)} %stack.2), calls=%async_computation | async-start | bytes 786432 | tf_op jit(solution)/shard_map/all_to_all | solution.py:50
  18.9 320.4 %reduce-scatter.2.cloned.1.call-start = ((), (), s32[]{:S(2)}) async-start(), calls=%async_computation.2 | async-start | bytes 13369344 | tf_op jit(solution)/shard_map/reduce_scatter | solution.py:57
Sparse Core Ops, SparseCore 0:
  211.6 127.6 reduce-scatter.1
